TPU v7x, 256 devices: a whole 4x4x8 slice. The times are simulated.
256 devices in a mesh: grp: 8 (over x, core), lx: 4 (over y), ly: 8 (over z).
Axes of the slice: x: 4, y: 4, z: 8, core: 2. Of those that a mesh axis runs over, the one named last changes fastest.
Arguments:
- vectors: float32 [32, 256, 4096], P('grp', 'lx', 'ly'), may hold values from -6 to 6
- levels: int32 [256, 4096], P('lx', 'ly'), may hold values from 0 to 7
- level_table: float32 [8], replicated, may hold values from 1 to 3
- filter_low: float32 [1], replicated, may hold values from -1 to 0.5
- filter_high: float32 [1], replicated, may hold values from 6 to 7.5
Outputs:
- basis: float32 [32, 256, 4096], P('grp', 'lx', 'ly')
All inputs are finite; a program needn't handle non-finite values.
Results may differ from a plain program's by a relative error of at most 0.00011.
Values sent between devices are 32-bit elements; how exact they have to be, the bound alone decides.
No kernel may reach another device: no remote copies, remote signals or barrier semaphores. Data moves between devices by JAX's collectives and lax.ppermute only.
A program may use at most 64 MiB of HBM per device.

v0:
```python
import jax
import jax.numpy as jnp
from jax import lax
from jax.sharding import PartitionSpec as P


def padded_2(shard, sides, width):
    for axis, dim in sides:
        size, length = (lax.axis_size(axis), shard.shape[dim])
        up = [(i, (i + 1) % size) for i in range(size)]
        down = [(j, i) for i, j in up]
        last = lax.slice_in_dim(shard, length - width, length, axis=dim)
        leading = lax.slice_in_dim(shard, 0, width, axis=dim)
        before = lax.ppermute(last, axis, up)
        after = lax.ppermute(leading, axis, down)
        shard = jnp.concatenate([before, shard, after], axis=dim)
    return shard


def from_root(value, axis, source):
    kept = jnp.where(lax.axis_index(axis) == source, value, 0).astype(value.dtype)
    return lax.psum(kept, axis)


def apply_operator(field, onsite):
    padded = padded_2(field, (("lx", 1), ("ly", 2)), 1)
    beside = padded[:, 2:, 1:-1] + padded[:, :-2, 1:-1] + padded[:, 1:-1, 2:] + padded[:, 1:-1, :-2]
    return onsite[None] * field - beside


def lower_inverse(gram):
    lower = jnp.linalg.cholesky(gram)
    eye_block = jnp.eye(gram.shape[0], dtype=jnp.float32)
    return lax.linalg.triangular_solve(lower, eye_block, left_side=True, lower=True)


def body(vectors, levels, level_table, filter_low, filter_high):
    count_vec, rows_local, cols_local = vectors.shape
    level_ids = jnp.arange(level_table.shape[0], dtype=jnp.int32)
    onsite = jnp.sum(
        jnp.where(levels[None] == level_ids[:, None, None], level_table[:, None, None], 0.0), axis=0
    )
    center = (filter_high[0] + filter_low[0]) / 2.0
    half = (filter_high[0] - filter_low[0]) / 2.0
    first = (apply_operator(vectors, onsite) - center * vectors) / half
    filtered = 2.0 * (apply_operator(first, onsite) - center * first) / half - vectors
    total = rows_local * cols_local * lax.axis_size("lx") * lax.axis_size("ly")
    flat = filtered.reshape(count_vec, rows_local * cols_local)
    highest = lax.Precision.HIGHEST
    mine = lax.axis_index("grp")
    result = jnp.zeros_like(flat)
    for h in range(lax.axis_size("grp")):
        gram = lax.psum(jnp.dot(flat, flat.T, precision=highest), ("lx", "ly")) / total
        done = jnp.dot(lower_inverse(gram), flat, precision=highest)
        result = jnp.where(mine == h, done, result)
        shared = from_root(done, "grp", h)
        coeff = lax.psum(jnp.dot(shared, flat.T, precision=highest), ("lx", "ly")) / total
        later = mine > h
        flat = jnp.where(later, flat - jnp.dot(coeff.T, shared, precision=highest), flat)
    return result.reshape(count_vec, rows_local, cols_local)


def solution(mesh):
    in_specs = (P("grp", "lx", "ly"), P("lx", "ly"), P(), P(), P())
    out_specs = P("grp", "lx", "ly")
    return jax.shard_map(body, mesh=mesh, in_specs=in_specs, out_specs=out_specs, check_vma=False)
```

profile of v0, /device:TPU:32, one launch (start us, length us, event | category | flops | bytes accessed | tf_op | source)
XLA Modules:
  0.0 1632.8 jit_solution(7607256732290742390)
XLA Ops:
  7.4 3.1 collective-permute-start
  11.9 3.5 collective-permute-done.1
  21.7 3.9 collective-permute-done.3
  26.2 2.0 collective-permute-start.5
  31.3 3.3 collective-permute-start.6
  34.6 2.7 collective-permute-done.6
  37.3 2.5 collective-permute-done.7
  40.2 2.4 convolution_bitcast_fusion
  42.6 71.0 %psum.154 = f32[4,4]{0,1:T(4,128)S(1)} all-reduce(f32[4,4]{0,1:T(4,128)S(1)} %convolution_bitcast_fusion), channel_id=1, replica_groups=mesh['grp'=8,'lx'=4,'ly'=8] {'lx','ly'}, use_global_device_ids=true, to_apply=%region_1.2 | all-reduce | flops 16 | bytes 128 | tf_op jit(solution)/shard_map/psum | solution.py:53
  118.3 60.3 %all-reduce.8.cloned.1.call-done = f32[4,32768]{1,0:T(4,128)} async-done(((f32[4,32768]{1,0:T(4,128)}), f32[4,32768]{1,0:T(4,128)}) %all-reduce.8.cloned.1.call-update) | async-done | bytes 524304 | tf_op jit(solution)/shard_map/psum | solution.py:22
  178.6 3.5 fusion.99
  182.1 71.6 %psum.156 = f32[4,4]{0,1:T(4,128)S(1)} all-reduce(f32[4,4]{0,1:T(4,128)S(1)} %fusion.99), channel_id=1, replica_groups=mesh['grp'=8,'lx'=4,'ly'=8] {'lx','ly'}, use_global_device_ids=true, to_apply=%region_5.8 | all-reduce | flops 16 | bytes 128 | tf_op jit(solution)/shard_map/psum | solution.py:57
  254.8 2.3 fusion.100
  257.1 73.6 %psum.157 = f32[4,4]{0,1:T(4,128)S(1)} all-reduce(f32[4,4]{0,1:T(4,128)S(1)} %fusion.100), channel_id=1, replica_groups=mesh['grp'=8,'lx'=4,'ly'=8] {'lx','ly'}, use_global_device_ids=true, to_apply=%region_6.9 | all-reduce | flops 16 | bytes 128 | tf_op jit(solution)/shard_map/psum | solution.py:53
  335.0 58.1 %all-reduce.10.cloned.1.call-done = f32[4,32768]{1,0:T(4,128)} async-done(((f32[4,32768]{1,0:T(4,128)}), f32[4,32768]{1,0:T(4,128)}) %all-reduce.10.cloned.1.call-update) | async-done | bytes 524304 | tf_op jit(solution)/shard_map/psum | solution.py:22
  393.1 3.5 fusion.101
  396.6 71.6 %psum.159 = f32[4,4]{0,1:T(4,128)S(1)} all-reduce(f32[4,4]{0,1:T(4,128)S(1)} %fusion.101), channel_id=1, replica_groups=mesh['grp'=8,'lx'=4,'ly'=8] {'lx','ly'}, use_global_device_ids=true, to_apply=%region_8.11 | all-reduce | flops 16 | bytes 128 | tf_op jit(solution)/shard_map/psum | solution.py:57
  469.2 2.3 fusion.102
  471.6 73.6 %psum.160 = f32[4,4]{0,1:T(4,128)S(1)} all-reduce(f32[4,4]{0,1:T(4,128)S(1)} %fusion.102), channel_id=1, replica_groups=mesh['grp'=8,'lx'=4,'ly'=8] {'lx','ly'}, use_global_device_ids=true, to_apply=%region_9.12 | all-reduce | flops 16 | bytes 128 | tf_op jit(solution)/shard_map/psum | solution.py:53
  549.8 57.8 %all-reduce.12.cloned.1.call-done = f32[4,32768]{1,0:T(4,128)} async-done(((f32[4,32768]{1,0:T(4,128)}), f32[4,32768]{1,0:T(4,128)}) %all-reduce.12.cloned.1.call-update) | async-done | bytes 524304 | tf_op jit(solution)/shard_map/psum | solution.py:22
  607.6 3.5 fusion.103
  611.1 71.6 %psum.162 = f32[4,4]{0,1:T(4,128)S(1)} all-reduce(f32[4,4]{0,1:T(4,128)S(1)} %fusion.103), channel_id=1, replica_groups=mesh['grp'=8,'lx'=4,'ly'=8] {'lx','ly'}, use_global_device_ids=true, to_apply=%region_11.14 | all-reduce | flops 16 | bytes 128 | tf_op jit(solution)/shard_map/psum | solution.py:57
  683.7 2.3 fusion.104
  686.1 73.6 %psum.163 = f32[4,4]{0,1:T(4,128)S(1)} all-reduce(f32[4,4]{0,1:T(4,128)S(1)} %fusion.104), channel_id=1, replica_groups=mesh['grp'=8,'lx'=4,'ly'=8] {'lx','ly'}, use_global_device_ids=true, to_apply=%region_12.15 | all-reduce | flops 16 | bytes 128 | tf_op jit(solution)/shard_map/psum | solution.py:53
  764.0 58.1 %all-reduce.14.cloned.1.call-done = f32[4,32768]{1,0:T(4,128)} async-done(((f32[4,32768]{1,0:T(4,128)}), f32[4,32768]{1,0:T(4,128)}) %all-reduce.14.cloned.1.call-update) | async-done | bytes 524304 | tf_op jit(solution)/shard_map/psum | solution.py:22
  822.1 3.5 fusion.105
  825.6 71.6 %psum.165 = f32[4,4]{0,1:T(4,128)S(1)} all-reduce(f32[4,4]{0,1:T(4,128)S(1)} %fusion.105), channel_id=1, replica_groups=mesh['grp'=8,'lx'=4,'ly'=8] {'lx','ly'}, use_global_device_ids=true, to_apply=%region_14.17 | all-reduce | flops 16 | bytes 128 | tf_op jit(solution)/shard_map/psum | solution.py:57
  898.2 2.3 fusion.106
  900.6 73.6 %psum.166 = f32[4,4]{0,1:T(4,128)S(1)} all-reduce(f32[4,4]{0,1:T(4,128)S(1)} %fusion.106), channel_id=1, replica_groups=mesh['grp'=8,'lx'=4,'ly'=8] {'lx','ly'}, use_global_device_ids=true, to_apply=%region_15.18 | all-reduce | flops 16 | bytes 128 | tf_op jit(solution)/shard_map/psum | solution.py:53
  978.9 57.6 %all-reduce.16.cloned.1.call-done = f32[4,32768]{1,0:T(4,128)} async-done(((f32[4,32768]{1,0:T(4,128)}), f32[4,32768]{1,0:T(4,128)}) %all-reduce.16.cloned.1.call-update) | async-done | bytes 524304 | tf_op jit(solution)/shard_map/psum | solution.py:22
  1036.6 3.5 fusion.107
  1040.0 71.6 %psum.168 = f32[4,4]{0,1:T(4,128)S(1)} all-reduce(f32[4,4]{0,1:T(4,128)S(1)} %fusion.107), channel_id=1, replica_groups=mesh['grp'=8,'lx'=4,'ly'=8] {'lx','ly'}, use_global_device_ids=true, to_apply=%region_17.20 | all-reduce | flops 16 | bytes 128 | tf_op jit(solution)/shard_map/psum | solution.py:57
  1111.6 2.0 fusion.2
  1113.7 2.3 fusion.108
  1116.0 73.6 %psum.169 = f32[4,4]{0,1:T(4,128)S(1)} all-reduce(f32[4,4]{0,1:T(4,128)S(1)} %fusion.108), channel_id=1, replica_groups=mesh['grp'=8,'lx'=4,'ly'=8] {'lx','ly'}, use_global_device_ids=true, to_apply=%region_18.21 | all-reduce | flops 16 | bytes 128 | tf_op jit(solution)/shard_map/psum | solution.py:53
  1192.1 2.0 broadcast_select_fusion.1
  1194.2 58.1 %all-reduce.18.cloned.1.call-done = f32[4,32768]{1,0:T(4,128)} async-done(((f32[4,32768]{1,0:T(4,128)}), f32[4,32768]{1,0:T(4,128)}) %all-reduce.18.cloned.1.call-update) | async-done | bytes 524304 | tf_op jit(solution)/shard_map/psum | solution.py:22
  1252.2 3.5 fusion.109
  1255.7 71.6 %psum.171 = f32[4,4]{0,1:T(4,128)S(1)} all-reduce(f32[4,4]{0,1:T(4,128)S(1)} %fusion.109), channel_id=1, replica_groups=mesh['grp'=8,'lx'=4,'ly'=8] {'lx','ly'}, use_global_device_ids=true, to_apply=%region_20.23 | all-reduce | flops 16 | bytes 128 | tf_op jit(solution)/shard_map/psum | solution.py:57
  1327.3 2.0 fusion.1
  1329.3 2.3 fusion.110
  1331.6 73.8 %psum.172 = f32[4,4]{0,1:T(4,128)S(1)} all-reduce(f32[4,4]{0,1:T(4,128)S(1)} %fusion.110), channel_id=1, replica_groups=mesh['grp'=8,'lx'=4,'ly'=8] {'lx','ly'}, use_global_device_ids=true, to_apply=%region_21.24 | all-reduce | flops 16 | bytes 128 | tf_op jit(solution)/shard_map/psum | solution.py:53
  1409.9 58.1 %all-reduce.20.cloned.1.call-done = f32[4,32768]{1,0:T(4,128)} async-done(((f32[4,32768]{1,0:T(4,128)}), f32[4,32768]{1,0:T(4,128)}) %all-reduce.20.cloned.1.call-update) | async-done | bytes 524304 | tf_op jit(solution)/shard_map/psum | solution.py:22
  1468.0 3.5 fusion.111
  1471.5 71.6 %psum.174 = f32[4,4]{0,1:T(4,128)S(1)} all-reduce(f32[4,4]{0,1:T(4,128)S(1)} %fusion.111), channel_id=1, replica_groups=mesh['grp'=8,'lx'=4,'ly'=8] {'lx','ly'}, use_global_device_ids=true, to_apply=%region_23.26 | all-reduce | flops 16 | bytes 128 | tf_op jit(solution)/shard_map/psum | solution.py:57
  1543.1 2.0 fusion
  1545.1 2.3 fusion.112
  1547.5 73.6 %psum.175 = f32[4,4]{0,1:T(4,128)S(1)} all-reduce(f32[4,4]{0,1:T(4,128)S(1)} %fusion.112), channel_id=1, replica_groups=mesh['grp'=8,'lx'=4,'ly'=8] {'lx','ly'}, use_global_device_ids=true, to_apply=%region_24.27 | all-reduce | flops 16 | bytes 128 | tf_op jit(solution)/shard_map/psum | solution.py:53
  (131 shorter events, 49.7 us)
Async XLA Ops:
  6.5 172.1 %all-reduce.8.cloned.1.call-start = ((), (), s32[]{:S(2)}) async-start(), calls=%async_computation | async-start | bytes 1048576 | tf_op jit(solution)/shard_map/psum | solution.py:22
  7.4 4.5 collective-permute-start
  10.5 8.1 copy-start.6
  10.5 15.1 copy-start
  10.5 4.9 collective-permute-start.1
  16.5 2.1 copy-start.7
  16.5 5.2 collective-permute-start.2
  16.7 9.0 collective-permute-start.3
  26.1 3.7 collective-permute-start.4
  26.2 4.9 collective-permute-start.5
  31.3 6.0 collective-permute-start.6
  34.6 5.1 collective-permute-start.7
  118.0 275.1 %all-reduce.10.cloned.1.call-start = ((), (), s32[]{:S(2)}) async-start(), calls=%async_computation.1 | async-start | bytes 1048576 | tf_op jit(solution)/shard_map/psum | solution.py:22
  178.6 75.1 %copy-start.5 = (f32[4,32768]{1,0:T(4,128)S(1)}, f32[4,32768]{1,0:T(4,128)}, u32[]{:S(2)}) copy-start(f32[4,32768]{1,0:T(4,128)} %all-reduce.8.cloned.1.call-done) | copy-start | bytes 1572868
  335.0 272.6 %all-reduce.12.cloned.1.call-start = ((), (), s32[]{:S(2)}) async-start(), calls=%async_computation.2 | async-start | bytes 1048576 | tf_op jit(solution)/shard_map/psum | solution.py:22
  393.1 75.1 %copy-start.2 = (f32[4,32768]{1,0:T(4,128)S(1)}, f32[4,32768]{1,0:T(4,128)}, u32[]{:S(2)}) copy-start(f32[4,32768]{1,0:T(4,128)} %all-reduce.10.cloned.1.call-done) | copy-start | bytes 1572868
  549.5 272.6 %all-reduce.14.cloned.1.call-start = ((), (), s32[]{:S(2)}) async-start(), calls=%async_computation.3 | async-start | bytes 1048576 | tf_op jit(solution)/shard_map/psum | solution.py:22
  607.6 75.1 %copy-start.3 = (f32[4,32768]{1,0:T(4,128)S(1)}, f32[4,32768]{1,0:T(4,128)}, u32[]{:S(2)}) copy-start(f32[4,32768]{1,0:T(4,128)} %all-reduce.12.cloned.1.call-done) | copy-start | bytes 1572868
  764.0 272.6 %all-reduce.16.cloned.1.call-start = ((), (), s32[]{:S(2)}) async-start(), calls=%async_computation.4 | async-start | bytes 1048576 | tf_op jit(solution)/shard_map/psum | solution.py:22
  822.1 75.1 %copy-start.4 = (f32[4,32768]{1,0:T(4,128)S(1)}, f32[4,32768]{1,0:T(4,128)}, u32[]{:S(2)}) copy-start(f32[4,32768]{1,0:T(4,128)} %all-reduce.14.cloned.1.call-done) | copy-start | bytes 1572868
  978.5 273.7 %all-reduce.18.cloned.1.call-start = ((), (), s32[]{:S(2)}) async-start(), calls=%async_computation.5 | async-start | bytes 1048576 | tf_op jit(solution)/shard_map/psum | solution.py:22
  1194.1 273.9 %all-reduce.20.cloned.1.call-start = ((), (), s32[]{:S(2)}) async-start(), calls=%async_computation.6 | async-start | bytes 1048576 | tf_op jit(solution)/shard_map/psum | solution.py:22
  1545.1 78.4 %copy-start.1 = (f32[4,32768]{1,0:T(4,128)S(1)}, f32[4,32768]{1,0:T(4,128)}, u32[]{:S(2)}) copy-start(f32[4,32768]{1,0:T(4,128)} %convolution_select_fusion.1) | copy-start | bytes 1572868
Sparse Core Ops, SparseCore 0:
  118.2 60.3 all-reduce.7
  335.1 57.9 all-reduce.9
  549.6 57.9 all-reduce.11
  764.1 57.9 all-reduce.13
  978.6 57.9 all-reduce.15
  1194.2 57.9 all-reduce.17
  1410.0 57.9 all-reduce.19
where the time goes:
time: 1640 us; the launch traced here: 1630 us
  blocking collectives  1090 us (66%)
  waiting for transfers between devices  427 us (26%)
  matrix products  69.2 us (4%)
  other arithmetic  19.4 us (1%)
    psum x8, blocking collectives, body(): lax.psum(jnp.dot(flat, flat.T, precision=highest), ('lx', 'ly')) / total  586 us
    psum x7, blocking collectives, body(): lax.psum(jnp.dot(shared, flat.T, precision=highest), ('lx', 'ly')) / total  501 us
    psum x7, waiting for transfers between devices, from_root(): return lax.psum(kept, axis)  408 us
  transfers between devices with their start and end apart: 15, of which 15 were waited for; matrix products, arithmetic and copies ran while one was open for 0% of the time, Pallas kernels for 0%

commit v1 on v0

--- a/solution.py
+++ b/solution.py
@@ -50,7 +50,7 @@
     mine = lax.axis_index("grp")
     result = jnp.zeros_like(flat)
     for h in range(lax.axis_size("grp")):
-        gram = lax.psum(jnp.dot(flat, flat.T, precision=highest), ("lx", "ly")) / total
+        gram = lax.psum(lax.psum(jnp.dot(flat, flat.T, precision=highest), "ly"), "lx") / total
         done = jnp.dot(lower_inverse(gram), flat, precision=highest)
         result = jnp.where(mine == h, done, result)
         shared = from_root(done, "grp", h)

time: 1640 us -> 1270 us (0.77)
  blocking collectives: 1090 us -> 706 us
    psum x8 -> x16, blocking collectives: 586 us -> 205 us  [the longest x8 142 us: body(): lax.psum(jnp.dot(flat, flat.T, precision=highest), 'ly')]
where the time goes in v1:
time: 1270 us; the launch traced here: 1260 us
  blocking collectives  706 us (56%)
  waiting for transfers between devices  437 us (34%)
  matrix products  69.2 us (5%)
  other arithmetic  19.4 us (2%)
  between operations  15.3 us (1%)
    psum x7, blocking collectives, body(): lax.psum(jnp.dot(shared, flat.T, precision=highest), ('lx', 'ly')) / total  501 us
    psum x7, waiting for transfers between devices, from_root(): return lax.psum(kept, axis)  419 us
    psum x8, blocking collectives, body(): lax.psum(jnp.dot(flat, flat.T, precision=highest), 'ly')  142 us
    psum x8, blocking collectives, body(): lax.psum(lax.psum(jnp.dot(flat, flat.T, precision=highest), 'ly'), 'lx')  62.7 us
  transfers between devices with their start and end apart: 15, of which 15 were waited for; matrix products, arithmetic and copies ran while one was open for 0% of the time, Pallas kernels for 0%

profile of v1, /device:TPU:32, one launch (start us, length us, event | category | flops | bytes accessed | tf_op | source)
XLA Modules:
  0.0 1262.1 jit_solution(12387116127768921658)
XLA Ops:
  7.4 3.1 collective-permute-start
  11.9 3.5 collective-permute-done.1
  21.7 3.9 collective-permute-done.3
  31.3 3.3 collective-permute-start.6
  34.6 2.7 collective-permute-done.6
  37.3 2.5 collective-permute-done.7
  40.2 2.4 convolution_bitcast_fusion
  42.6 15.4 %psum.210 = f32[4,4]{0,1:T(4,128)S(1)} all-reduce(f32[4,4]{0,1:T(4,128)S(1)} %convolution_bitcast_fusion), channel_id=1, replica_groups=mesh['grp'=8,'lx'=4,'ly'=8] {'ly'}, use_global_device_ids=true, to_apply=%region_1.2 | all-reduce | flops 16 | bytes 128 | tf_op jit(solution)/shard_map/psum | solution.py:53
  58.0 8.4 psum.211
  71.2 62.1 %all-reduce.8.cloned.1.call-done = f32[4,32768]{1,0:T(4,128)} async-done(((f32[4,32768]{1,0:T(4,128)}), f32[4,32768]{1,0:T(4,128)}) %all-reduce.8.cloned.1.call-update) | async-done | bytes 524304 | tf_op jit(solution)/shard_map/psum | solution.py:22
  133.3 3.5 fusion.99
  136.9 71.6 %psum.213 = f32[4,4]{0,1:T(4,128)S(1)} all-reduce(f32[4,4]{0,1:T(4,128)S(1)} %fusion.99), channel_id=1, replica_groups=mesh['grp'=8,'lx'=4,'ly'=8] {'lx','ly'}, use_global_device_ids=true, to_apply=%region_6.9 | all-reduce | flops 16 | bytes 128 | tf_op jit(solution)/shard_map/psum | solution.py:57
  209.5 2.3 fusion.100
  211.8 18.1 %psum.214 = f32[4,4]{0,1:T(4,128)S(1)} all-reduce(f32[4,4]{0,1:T(4,128)S(1)} %fusion.100), channel_id=1, replica_groups=mesh['grp'=8,'lx'=4,'ly'=8] {'ly'}, use_global_device_ids=true, to_apply=%region_7.10 | all-reduce | flops 16 | bytes 128 | tf_op jit(solution)/shard_map/psum | solution.py:53
  229.9 7.7 psum.215
  242.0 59.5 %all-reduce.10.cloned.1.call-done = f32[4,32768]{1,0:T(4,128)} async-done(((f32[4,32768]{1,0:T(4,128)}), f32[4,32768]{1,0:T(4,128)}) %all-reduce.10.cloned.1.call-update) | async-done | bytes 524304 | tf_op jit(solution)/shard_map/psum | solution.py:22
  301.6 3.5 fusion.101
  305.1 71.6 %psum.217 = f32[4,4]{0,1:T(4,128)S(1)} all-reduce(f32[4,4]{0,1:T(4,128)S(1)} %fusion.101), channel_id=1, replica_groups=mesh['grp'=8,'lx'=4,'ly'=8] {'lx','ly'}, use_global_device_ids=true, to_apply=%region_10.13 | all-reduce | flops 16 | bytes 128 | tf_op jit(solution)/shard_map/psum | solution.py:57
  380.0 18.1 %psum.218 = f32[4,4]{0,1:T(4,128)S(1)} all-reduce(f32[4,4]{0,1:T(4,128)S(1)} %fusion.102), channel_id=1, replica_groups=mesh['grp'=8,'lx'=4,'ly'=8] {'ly'}, use_global_device_ids=true, to_apply=%region_11.14 | all-reduce | flops 16 | bytes 128 | tf_op jit(solution)/shard_map/psum | solution.py:53
  398.1 7.7 psum.219
  410.5 59.3 %all-reduce.12.cloned.1.call-done = f32[4,32768]{1,0:T(4,128)} async-done(((f32[4,32768]{1,0:T(4,128)}), f32[4,32768]{1,0:T(4,128)}) %all-reduce.12.cloned.1.call-update) | async-done | bytes 524304 | tf_op jit(solution)/shard_map/psum | solution.py:22
  469.7 3.5 fusion.103
  473.3 71.6 %psum.221 = f32[4,4]{0,1:T(4,128)S(1)} all-reduce(f32[4,4]{0,1:T(4,128)S(1)} %fusion.103), channel_id=1, replica_groups=mesh['grp'=8,'lx'=4,'ly'=8] {'lx','ly'}, use_global_device_ids=true, to_apply=%region_14.17 | all-reduce | flops 16 | bytes 128 | tf_op jit(solution)/shard_map/psum | solution.py:57
  548.2 18.1 %psum.222 = f32[4,4]{0,1:T(4,128)S(1)} all-reduce(f32[4,4]{0,1:T(4,128)S(1)} %fusion.104), channel_id=1, replica_groups=mesh['grp'=8,'lx'=4,'ly'=8] {'ly'}, use_global_device_ids=true, to_apply=%region_15.18 | all-reduce | flops 16 | bytes 128 | tf_op jit(solution)/shard_map/psum | solution.py:53
  566.3 7.7 psum.223
  578.4 59.5 %all-reduce.14.cloned.1.call-done = f32[4,32768]{1,0:T(4,128)} async-done(((f32[4,32768]{1,0:T(4,128)}), f32[4,32768]{1,0:T(4,128)}) %all-reduce.14.cloned.1.call-update) | async-done | bytes 524304 | tf_op jit(solution)/shard_map/psum | solution.py:22
  637.9 3.5 fusion.105
  641.5 71.6 %psum.225 = f32[4,4]{0,1:T(4,128)S(1)} all-reduce(f32[4,4]{0,1:T(4,128)S(1)} %fusion.105), channel_id=1, replica_groups=mesh['grp'=8,'lx'=4,'ly'=8] {'lx','ly'}, use_global_device_ids=true, to_apply=%region_18.21 | all-reduce | flops 16 | bytes 128 | tf_op jit(solution)/shard_map/psum | solution.py:57
  714.1 2.3 fusion.106
  716.4 18.1 %psum.226 = f32[4,4]{0,1:T(4,128)S(1)} all-reduce(f32[4,4]{0,1:T(4,128)S(1)} %fusion.106), channel_id=1, replica_groups=mesh['grp'=8,'lx'=4,'ly'=8] {'ly'}, use_global_device_ids=true, to_apply=%region_19.22 | all-reduce | flops 16 | bytes 128 | tf_op jit(solution)/shard_map/psum | solution.py:53
  734.5 7.7 psum.227
  747.0 59.1 %all-reduce.16.cloned.1.call-done = f32[4,32768]{1,0:T(4,128)} async-done(((f32[4,32768]{1,0:T(4,128)}), f32[4,32768]{1,0:T(4,128)}) %all-reduce.16.cloned.1.call-update) | async-done | bytes 524304 | tf_op jit(solution)/shard_map/psum | solution.py:22
  806.1 3.5 fusion.107
  809.6 71.6 %psum.229 = f32[4,4]{0,1:T(4,128)S(1)} all-reduce(f32[4,4]{0,1:T(4,128)S(1)} %fusion.107), channel_id=1, replica_groups=mesh['grp'=8,'lx'=4,'ly'=8] {'lx','ly'}, use_global_device_ids=true, to_apply=%region_22.25 | all-reduce | flops 16 | bytes 128 | tf_op jit(solution)/shard_map/psum | solution.py:57
  883.2 2.3 fusion.108
  885.6 18.1 %psum.230 = f32[4,4]{0,1:T(4,128)S(1)} all-reduce(f32[4,4]{0,1:T(4,128)S(1)} %fusion.108), channel_id=1, replica_groups=mesh['grp'=8,'lx'=4,'ly'=8] {'ly'}, use_global_device_ids=true, to_apply=%region_23.26 | all-reduce | flops 16 | bytes 128 | tf_op jit(solution)/shard_map/psum | solution.py:53
  903.7 7.7 psum.231
  916.0 59.6 %all-reduce.18.cloned.1.call-done = f32[4,32768]{1,0:T(4,128)} async-done(((f32[4,32768]{1,0:T(4,128)}), f32[4,32768]{1,0:T(4,128)}) %all-reduce.18.cloned.1.call-update) | async-done | bytes 524304 | tf_op jit(solution)/shard_map/psum | solution.py:22
  975.5 3.5 fusion.109
  979.0 71.6 %psum.233 = f32[4,4]{0,1:T(4,128)S(1)} all-reduce(f32[4,4]{0,1:T(4,128)S(1)} %fusion.109), channel_id=1, replica_groups=mesh['grp'=8,'lx'=4,'ly'=8] {'lx','ly'}, use_global_device_ids=true, to_apply=%region_26.29 | all-reduce | flops 16 | bytes 128 | tf_op jit(solution)/shard_map/psum | solution.py:57
  1055.0 18.1 %psum.234 = f32[4,4]{0,1:T(4,128)S(1)} all-reduce(f32[4,4]{0,1:T(4,128)S(1)} %fusion.110), channel_id=1, replica_groups=mesh['grp'=8,'lx'=4,'ly'=8] {'ly'}, use_global_device_ids=true, to_apply=%region_27.30 | all-reduce | flops 16 | bytes 128 | tf_op jit(solution)/shard_map/psum | solution.py:53
  1073.1 7.9 psum.235
  1085.5 59.6 %all-reduce.20.cloned.1.call-done = f32[4,32768]{1,0:T(4,128)} async-done(((f32[4,32768]{1,0:T(4,128)}), f32[4,32768]{1,0:T(4,128)}) %all-reduce.20.cloned.1.call-update) | async-done | bytes 524304 | tf_op jit(solution)/shard_map/psum | solution.py:22
  1145.1 3.5 fusion.111
  1148.5 71.6 %psum.237 = f32[4,4]{0,1:T(4,128)S(1)} all-reduce(f32[4,4]{0,1:T(4,128)S(1)} %fusion.111), channel_id=1, replica_groups=mesh['grp'=8,'lx'=4,'ly'=8] {'lx','ly'}, use_global_device_ids=true, to_apply=%region_30.33 | all-reduce | flops 16 | bytes 128 | tf_op jit(solution)/shard_map/psum | solution.py:57
  1222.2 2.3 fusion.112
  1224.5 18.1 %psum.238 = f32[4,4]{0,1:T(4,128)S(1)} all-reduce(f32[4,4]{0,1:T(4,128)S(1)} %fusion.112), channel_id=1, replica_groups=mesh['grp'=8,'lx'=4,'ly'=8] {'ly'}, use_global_device_ids=true, to_apply=%region_31.34 | all-reduce | flops 16 | bytes 128 | tf_op jit(solution)/shard_map/psum | solution.py:53
  1242.6 7.7 psum.239
  (139 shorter events, 66.8 us)
Async XLA Ops:
  6.5 126.8 %all-reduce.8.cloned.1.call-start = ((), (), s32[]{:S(2)}) async-start(), calls=%async_computation | async-start | bytes 1048576 | tf_op jit(solution)/shard_map/psum | solution.py:22
  7.4 4.5 collective-permute-start
  10.5 8.1 copy-start.6
  10.5 15.1 %copy-start = (f32[4,64,512]{2,1,0:T(8,128)S(1)}, f32[4,64,512]{2,1,0:T(8,128)}, u32[]{:S(2)}) copy-start(f32[4,64,512]{2,1,0:T(8,128)} %param.8) | copy-start | bytes 1572868
  10.5 4.9 collective-permute-start.1
  16.5 2.1 copy-start.7
  16.5 5.2 collective-permute-start.2
  16.7 9.0 collective-permute-start.3
  26.1 3.7 collective-permute-start.4
  26.2 4.9 collective-permute-start.5
  31.3 6.0 collective-permute-start.6
  34.6 5.1 collective-permute-start.7
  71.0 230.6 %all-reduce.10.cloned.1.call-start = ((), (), s32[]{:S(2)}) async-start(), calls=%async_computation.1 | async-start | bytes 1048576 | tf_op jit(solution)/shard_map/psum | solution.py:22
  133.3 75.1 %copy-start.5 = (f32[4,32768]{1,0:T(4,128)S(1)}, f32[4,32768]{1,0:T(4,128)}, u32[]{:S(2)}) copy-start(f32[4,32768]{1,0:T(4,128)} %all-reduce.8.cloned.1.call-done) | copy-start | bytes 1572868
  242.0 227.8 %all-reduce.12.cloned.1.call-start = ((), (), s32[]{:S(2)}) async-start(), calls=%async_computation.2 | async-start | bytes 1048576 | tf_op jit(solution)/shard_map/psum | solution.py:22
  301.6 75.1 %copy-start.2 = (f32[4,32768]{1,0:T(4,128)S(1)}, f32[4,32768]{1,0:T(4,128)}, u32[]{:S(2)}) copy-start(f32[4,32768]{1,0:T(4,128)} %all-reduce.10.cloned.1.call-done) | copy-start | bytes 1572868
  410.2 227.8 %all-reduce.14.cloned.1.call-start = ((), (), s32[]{:S(2)}) async-start(), calls=%async_computation.3 | async-start | bytes 1048576 | tf_op jit(solution)/shard_map/psum | solution.py:22
  469.7 75.1 %copy-start.3 = (f32[4,32768]{1,0:T(4,128)S(1)}, f32[4,32768]{1,0:T(4,128)}, u32[]{:S(2)}) copy-start(f32[4,32768]{1,0:T(4,128)} %all-reduce.12.cloned.1.call-done) | copy-start | bytes 1572868
  578.4 227.8 %all-reduce.16.cloned.1.call-start = ((), (), s32[]{:S(2)}) async-start(), calls=%async_computation.4 | async-start | bytes 1048576 | tf_op jit(solution)/shard_map/psum | solution.py:22
  637.9 75.1 %copy-start.4 = (f32[4,32768]{1,0:T(4,128)S(1)}, f32[4,32768]{1,0:T(4,128)}, u32[]{:S(2)}) copy-start(f32[4,32768]{1,0:T(4,128)} %all-reduce.14.cloned.1.call-done) | copy-start | bytes 1572868
  746.6 228.9 %all-reduce.18.cloned.1.call-start = ((), (), s32[]{:S(2)}) async-start(), calls=%async_computation.5 | async-start | bytes 1048576 | tf_op jit(solution)/shard_map/psum | solution.py:22
  915.9 229.2 %all-reduce.20.cloned.1.call-start = ((), (), s32[]{:S(2)}) async-start(), calls=%async_computation.6 | async-start | bytes 1048576 | tf_op jit(solution)/shard_map/psum | solution.py:22
  1222.2 30.7 %copy-start.1 = (f32[4,32768]{1,0:T(4,128)S(1)}, f32[4,32768]{1,0:T(4,128)}, u32[]{:S(2)}) copy-start(f32[4,32768]{1,0:T(4,128)} %convolution_select_fusion.1) | copy-start | bytes 1572868
Sparse Core Ops, SparseCore 0:
  71.1 62.2 all-reduce.7
  242.1 59.3 all-reduce.9
  410.3 59.3 all-reduce.11
  578.5 59.3 all-reduce.13
  746.7 59.3 all-reduce.15
  916.0 59.4 all-reduce.17
  1085.6 59.4 all-reduce.19
